TPU v7x, 32 devices: a whole 2x2x4 slice. The times are simulated.
32 devices in a mesh: rows: 4 (over y, x), cols: 8 (over z, core).
Axes of the slice: x: 2, y: 2, z: 4, core: 2. Of those that a mesh axis runs over, the one named last changes fastest.
Arguments:
- data_tile: bfloat16 [1024, 8192], P('rows', 'cols'), may hold values from 0.05 to 5
- w_factor: float32 [32, 1024], P(None, ('rows', 'cols')), may hold values from 0.05 to 0.5
- h_factor: float32 [32, 8192], P(None, ('cols', 'rows')), may hold values from 0.05 to 0.5
Outputs:
- w_final: float32 [32, 1024], P(None, ('rows', 'cols'))
- h_final: float32 [32, 8192], P(None, ('cols', 'rows'))
All inputs are finite; a program needn't handle non-finite values.
Results may differ from a plain program's by a relative error of at most 0.00049.
Values may be sent and summed in bfloat16 or wider, within the bound.
A program may use at most 64 MiB of HBM per device.

v0:
```python
import jax
import jax.numpy as jnp
from jax import lax
from jax.sharding import PartitionSpec as P

ITERS = 2
damping = 0.75


def quotient_terms(data_tile, w_block, h_block):
    approx = jnp.einsum("ki,kj->ij", w_block, h_block, preferred_element_type=jnp.float32)
    quotient = (data_tile.astype(jnp.float32) / approx).astype(jnp.bfloat16)
    h_part = jnp.einsum("ki,ij->kj", w_block, quotient, preferred_element_type=jnp.float32)
    w_part = jnp.einsum("kj,ij->ki", h_block, quotient, preferred_element_type=jnp.float32)
    return (h_part, w_part)


def row_sums(block):
    return jnp.sum(block.astype(jnp.float32), axis=1)


def totals(w_own, h_own):
    w_total, h_total = lax.psum((row_sums(w_own), row_sums(h_own)), ("rows", "cols"))
    return (w_total, h_total)


def scaled(factor, numer, total):
    return factor * (1.0 - damping + damping * numer / total[:, None])


def shards(data_tile, w_factor, h_factor):
    w_now = w_factor
    h_now = h_factor
    for rounds in range(ITERS):
        w_round = w_now.astype(jnp.bfloat16)
        h_round = h_now.astype(jnp.bfloat16)
        w_block = lax.all_gather(w_round, "cols", axis=1, tiled=True)
        h_block = lax.all_gather(h_round, "rows", axis=1, tiled=True)
        h_part, w_part = quotient_terms(data_tile, w_block, h_block)
        h_numer = lax.psum_scatter(h_part, "rows", scatter_dimension=1, tiled=True)
        w_numer = lax.psum_scatter(w_part, "cols", scatter_dimension=1, tiled=True)
        w_total, h_total = totals(w_round, h_round)
        h_next = scaled(h_now, h_numer, w_total)
        w_next = scaled(w_now, w_numer, h_total)
        w_now = w_next
        h_now = h_next
    return (w_now, h_now)


def solution(mesh):
    placed = (P("rows", "cols"), P(None, ("rows", "cols")), P(None, ("cols", "rows")))
    return jax.shard_map(
        shards,
        mesh=mesh,
        in_specs=placed,
        out_specs=(P(None, ("rows", "cols")), P(None, ("cols", "rows"))),
        check_vma=False,
    )
```

profile of v0, /device:TPU:0, one launch (start us, length us, event | category | flops | bytes accessed | tf_op | source)
XLA Modules:
  0.0 165.2 jit_solution(12160451287689017585)
XLA Ops:
  7.2 0.9 convert_reduce_fusion.1
  8.1 10.1 %all_gather.13 = bf16[32,1024]{1,0:T(8,128)(2,1)S(1)} all-gather(bf16[32,256]{1,0:T(8,128)(2,1)S(1)} %get-tuple-element.11), channel_id=1, replica_groups=mesh['rows'=4,'cols'=8] {'rows'}, dimensions={1}, use_global_device_ids=true | all-gather | bytes 81920 | tf_op jit(solution)/shard_map/all_gather | solution.py:38
  18.2 0.1 copy.5
  18.2 14.2 %all_gather.12 = bf16[32,256]{0,1:T(8,128)(2,1)S(1)} all-gather(bf16[32,32]{0,1:T(8,128)(2,1)S(1)} %copy.5), channel_id=1, replica_groups=mesh['rows'=4,'cols'=8] {'cols'}, dimensions={1}, use_global_device_ids=true | all-gather | bytes 18432 | tf_op jit(solution)/shard_map/all_gather | solution.py:37
  32.4 1.3 fusion
  33.8 0.2 convolution_bitcast_fusion.2
  34.0 0.8 copy.7
  34.9 0.9 convolution_bitcast_fusion.1
  35.9 39.3 %all-reduce.1 = (f32[32]{0:T(128)S(1)}, f32[32]{0:T(128)S(1)}) all-reduce(f32[32]{0:T(128)S(1)} %convert_reduce_fusion.3, f32[32]{0:T(128)S(1)} %get-tuple-element.10), channel_id=1, replica_groups=mesh['rows'=4,'cols'=8] {'rows','cols'}, use_global_device_ids=true, to_apply=%region_5.0 | all-reduce | flops 64 | bytes 512 | tf_op jit(solution)/shard_map/psum | solution.py:23
  75.2 0.8 copy.8
  76.0 0.2 convert_reduce_fusion.2
  76.2 0.1 copy.6
  76.2 14.1 %all_gather.15 = bf16[32,256]{0,1:T(8,128)(2,1)S(1)} all-gather(bf16[32,32]{0,1:T(8,128)(2,1)S(1)} %copy.6), channel_id=1, replica_groups=mesh['rows'=4,'cols'=8] {'cols'}, dimensions={1}, use_global_device_ids=true | all-gather | bytes 18432 | tf_op jit(solution)/shard_map/all_gather | solution.py:37
  90.4 0.4 reduce-scatter.9.cloned.1.call-done
  90.8 0.9 convert_reduce_fusion
  91.7 8.8 %all_gather.14 = bf16[32,1024]{1,0:T(8,128)(2,1)S(1)} all-gather(bf16[32,256]{1,0:T(8,128)(2,1)S(1)} %get-tuple-element.9), channel_id=1, replica_groups=mesh['rows'=4,'cols'=8] {'rows'}, dimensions={1}, use_global_device_ids=true | all-gather | bytes 81920 | tf_op jit(solution)/shard_map/all_gather | solution.py:38
  100.5 0.3 fusion.1
  100.8 0.9 convolution_bitcast_fusion
  101.8 0.9 fusion.6
  102.7 39.0 %all-reduce = (f32[32]{0:T(128)S(1)}, f32[32]{0:T(128)S(1)}) all-reduce(f32[32]{0:T(128)S(1)} %get-tuple-element.8, f32[32]{0:T(128)S(1)} %get-tuple-element.6), channel_id=1, replica_groups=mesh['rows'=4,'cols'=8] {'rows','cols'}, use_global_device_ids=true, to_apply=%region_8.0 | all-reduce | flops 64 | bytes 512 | tf_op jit(solution)/shard_map/psum | solution.py:23
  141.7 0.8 copy.10
  142.5 0.7 add_multiply_fusion.2
  143.2 14.1 %reduce-scatter.11.cloned.1.call-done = f32[32,256]{1,0:T(8,128)} async-done(((f32[32,1024]{1,0:T(8,128)}), f32[32,256]{1,0:T(8,128)}) %reduce-scatter.11.cloned.1.call-update) | async-done | bytes 32784 | tf_op jit(solution)/shard_map/reduce_scatter | solution.py:40
  157.2 1.5 add_multiply_fusion
  (19 shorter events, 0.3 us)
Async XLA Ops:
  7.2 68.0 %reduce-scatter.13.cloned.1.call-start = ((), (), s32[]{:S(2)}) async-start(), calls=%async_computation.6 | async-start | bytes 147456
  8.1 10.1 %copy-start.1 = (f32[32,32]{1,0:T(8,128)S(1)}, f32[32,32]{1,0:T(8,128)}, u32[]{:S(2)}) copy-start(f32[32,32]{1,0:T(8,128)} %param.4) | copy-start | bytes 12292
  34.8 65.7 %copy-start.3 = (bf16[256,1024]{1,0:T(8,128)(2,1)S(1)}, bf16[256,1024]{1,0:T(8,128)(2,1)}, u32[]{:S(2)}) copy-start(bf16[256,1024]{1,0:T(8,128)(2,1)} %param.3) | copy-start | bytes 1572868
  34.8 55.9 %reduce-scatter.9.cloned.1.call-start = ((), (), s32[]{:S(2)}) async-start(), calls=%async_computation.4 | async-start | bytes 163840 | tf_op jit(solution)/shard_map/reduce_scatter | solution.py:40
  35.8 105.9 %reduce-scatter.15.cloned.1.call-start = ((), (), s32[]{:S(2)}) async-start(), calls=%async_computation.7 | async-start | bytes 147456
  76.2 14.5 %copy-start = (f32[32,256]{1,0:T(8,128)S(1)}, f32[32,256]{1,0:T(8,128)}, u32[]{:S(2)}) copy-start(f32[32,256]{1,0:T(8,128)} %param.5) | copy-start | bytes 98308
  101.7 55.5 %reduce-scatter.11.cloned.1.call-start = ((), (), s32[]{:S(2)}) async-start(), calls=%async_computation.5 | async-start | bytes 163840 | tf_op jit(solution)/shard_map/reduce_scatter | solution.py:40
  142.5 14.8 %copy-start.2 = (f32[32,256]{1,0:T(8,128)S(1)}, f32[32,256]{1,0:T(8,128)}, u32[]{:S(2)}) copy-start(f32[32,256]{1,0:T(8,128)} %reduce-scatter.9.cloned.1.call-done) | copy-start | bytes 98308
Sparse Core Ops, SparseCore 0:
  34.9 30.7 reduce-scatter.12
  68.4 22.2 reduce-scatter.8
  101.9 30.2 reduce-scatter.14
  134.7 22.4 reduce-scatter.10
where the time goes:
time: 166 us; the launch traced here: 165 us
  blocking collectives  126 us (76%)
  waiting for transfers between devices  14.5 us (9%)
  between operations  13.8 us (8%)
  matrix products  4.5 us (3%)
  other arithmetic  4.17 us (3%)
  local copies, waits for them, and re-layouts  2.53 us (2%)
    psum x2, blocking collectives, totals(): lax.psum((row_sums(w_own), row_sums(h_own)), ('rows', 'cols'))  78.3 us
    all_gather x2, blocking collectives, shards(): w_block = lax.all_gather(w_round, 'cols', axis=1, tiled=True)  28.3 us
    all_gather x2, blocking collectives, shards(): h_block = lax.all_gather(h_round, 'rows', axis=1, tiled=True)  18.9 us
    reduce_scatter x2, waiting for transfers between devices, shards(): h_numer = lax.psum_scatter(h_part, 'rows', scatter_dimension=1, tiled=True)  14.5 us
  transfers between devices with their start and end apart: 4, of which 2 were waited for; matrix products, arithmetic and copies ran while one was open for 3% of the time, Pallas kernels for 0%

commit v1 on v0

--- a/solution.py
+++ b/solution.py
@@ -34,7 +34,7 @@
     for rounds in range(ITERS):
         w_round = w_now.astype(jnp.bfloat16)
         h_round = h_now.astype(jnp.bfloat16)
-        w_block = lax.all_gather(w_round, "cols", axis=1, tiled=True)
+        w_block = jnp.concatenate(lax.all_gather(w_round, "cols"), axis=1)
         h_block = lax.all_gather(h_round, "rows", axis=1, tiled=True)
         h_part, w_part = quotient_terms(data_tile, w_block, h_block)
         h_numer = lax.psum_scatter(h_part, "rows", scatter_dimension=1, tiled=True)

time: 166 us -> 167 us (level)
  no operation moved by 1% of the time
where the time goes in v1:
time: 167 us; the launch traced here: 166 us
  blocking collectives  125 us (75%)
  waiting for transfers between devices  14.5 us (9%)
  between operations  13.8 us (8%)
  other arithmetic  4.98 us (3%)
  matrix products  4.57 us (3%)
  local copies, waits for them, and re-layouts  2.77 us (2%)
    psum x2, blocking collectives, totals(): lax.psum((row_sums(w_own), row_sums(h_own)), ('rows', 'cols'))  77.7 us
    all_gather x2, blocking collectives, shards(): w_block = jnp.concatenate(lax.all_gather(w_round, 'cols'), axis=1)  29.7 us
    all_gather x2, blocking collectives, shards(): h_block = lax.all_gather(h_round, 'rows', axis=1, tiled=True)  17.7 us
    reduce_scatter x2, waiting for transfers between devices, shards(): h_numer = lax.psum_scatter(h_part, 'rows', scatter_dimension=1, tiled=True)  14.4 us
  transfers between devices with their start and end apart: 4, of which 2 were waited for; matrix products, arithmetic and copies ran while one was open for 3% of the time, Pallas kernels for 0%

profile of v1, /device:TPU:0, one launch (start us, length us, event | category | flops | bytes accessed | tf_op | source)
XLA Modules:
  0.0 165.9 jit_solution(5111842173575938902)
XLA Ops:
  7.2 0.8 convert_reduce_fusion.3
  8.0 0.9 convert_reduce_fusion.1
  8.9 15.7 %all-gather = bf16[256,32]{1,0:T(8,128)(2,1)S(1)} all-gather(bf16[32,32]{1,0:T(8,128)(2,1)S(1)} %get-tuple-element.13), channel_id=2, replica_groups=mesh['rows'=4,'cols'=8] {'cols'}, dimensions={0}, use_global_device_ids=true | all-gather | bytes 18432 | tf_op jit(solution)/shard_map/all_gather | solution.py:37
  24.7 8.5 %all_gather.20 = bf16[32,1024]{1,0:T(8,128)(2,1)S(1)} all-gather(bf16[32,256]{1,0:T(8,128)(2,1)S(1)} %get-tuple-element.11), channel_id=1, replica_groups=mesh['rows'=4,'cols'=8] {'rows'}, dimensions={1}, use_global_device_ids=true | all-gather | bytes 81920 | tf_op jit(solution)/shard_map/all_gather | solution.py:38
  33.2 1.4 fusion
  34.6 0.3 convolution_bitcast_fusion.2
  34.8 0.8 copy.9
  35.7 0.8 convolution_bitcast_fusion
  36.6 39.3 %all-reduce.1 = (f32[32]{0:T(128)S(1)}, f32[32]{0:T(128)S(1)}) all-reduce(f32[32]{0:T(128)S(1)} %get-tuple-element.12, f32[32]{0:T(128)S(1)} %get-tuple-element.10), channel_id=1, replica_groups=mesh['rows'=4,'cols'=8] {'rows','cols'}, use_global_device_ids=true, to_apply=%region_5.0 | all-reduce | flops 64 | bytes 512 | tf_op jit(solution)/shard_map/psum | solution.py:23
  75.9 0.8 copy.10
  76.7 0.2 convert_reduce_fusion.2
  76.9 14.0 %all-gather.1 = bf16[256,32]{1,0:T(8,128)(2,1)S(1)} all-gather(bf16[32,32]{1,0:T(8,128)(2,1)S(1)} %get-tuple-element.7), channel_id=3, replica_groups=mesh['rows'=4,'cols'=8] {'cols'}, dimensions={0}, use_global_device_ids=true | all-gather | bytes 18432 | tf_op jit(solution)/shard_map/all_gather | solution.py:37
  91.1 0.5 reduce-scatter.9.cloned.1.call-done
  91.6 0.1 copy-done
  91.7 0.9 convert_reduce_fusion
  92.7 9.2 %all_gather.21 = bf16[32,1024]{1,0:T(8,128)(2,1)S(1)} all-gather(bf16[32,256]{1,0:T(8,128)(2,1)S(1)} %get-tuple-element.9), channel_id=1, replica_groups=mesh['rows'=4,'cols'=8] {'rows'}, dimensions={1}, use_global_device_ids=true | all-gather | bytes 81920 | tf_op jit(solution)/shard_map/all_gather | solution.py:38
  101.9 0.3 fusion.1
  102.2 0.9 convolution_bitcast_fusion.1
  103.2 0.9 fusion.6
  104.1 38.4 %all-reduce = (f32[32]{0:T(128)S(1)}, f32[32]{0:T(128)S(1)}) all-reduce(f32[32]{0:T(128)S(1)} %get-tuple-element.8, f32[32]{0:T(128)S(1)} %get-tuple-element.6), channel_id=1, replica_groups=mesh['rows'=4,'cols'=8] {'rows','cols'}, use_global_device_ids=true, to_apply=%region_8.0 | all-reduce | flops 64 | bytes 512 | tf_op jit(solution)/shard_map/psum | solution.py:23
  142.5 0.8 copy.12
  143.3 0.7 add_multiply_fusion.2
  144.0 13.9 %reduce-scatter.11.cloned.1.call-done = f32[32,256]{1,0:T(8,128)} async-done(((f32[32,1024]{1,0:T(8,128)}), f32[32,256]{1,0:T(8,128)}) %reduce-scatter.11.cloned.1.call-update) | async-done | bytes 32784 | tf_op jit(solution)/shard_map/reduce_scatter | solution.py:40
  157.9 1.5 add_multiply_fusion
  (21 shorter events, 0.5 us)
Async XLA Ops:
  7.2 68.8 %reduce-scatter.13.cloned.1.call-start = ((), (), s32[]{:S(2)}) async-start(), calls=%async_computation.6 | async-start | bytes 147456
  35.6 66.2 %copy-start.3 = (bf16[256,1024]{1,0:T(8,128)(2,1)S(1)}, bf16[256,1024]{1,0:T(8,128)(2,1)}, u32[]{:S(2)}) copy-start(bf16[256,1024]{1,0:T(8,128)(2,1)} %param.3) | copy-start | bytes 1572868
  35.6 55.9 %reduce-scatter.9.cloned.1.call-start = ((), (), s32[]{:S(2)}) async-start(), calls=%async_computation.4 | async-start | bytes 163840 | tf_op jit(solution)/shard_map/reduce_scatter | solution.py:40
  36.5 105.9 %reduce-scatter.15.cloned.1.call-start = ((), (), s32[]{:S(2)}) async-start(), calls=%async_computation.7 | async-start | bytes 147456
  75.9 0.8 copy-start.1
  90.9 0.8 copy-start
  103.1 54.7 %reduce-scatter.11.cloned.1.call-start = ((), (), s32[]{:S(2)}) async-start(), calls=%async_computation.5 | async-start | bytes 163840 | tf_op jit(solution)/shard_map/reduce_scatter | solution.py:40
  143.3 14.6 %copy-start.2 = (f32[32,256]{1,0:T(8,128)S(1)}, f32[32,256]{1,0:T(8,128)}, u32[]{:S(2)}) copy-start(f32[32,256]{1,0:T(8,128)} %reduce-scatter.9.cloned.1.call-done) | copy-start | bytes 98308
Sparse Core Ops, SparseCore 0:
  35.7 30.6 reduce-scatter.12
  69.2 22.3 reduce-scatter.8
  103.3 29.6 reduce-scatter.14
  135.6 22.2 reduce-scatter.10
